TPU v7x, 256 devices: a whole 4x4x8 slice. The times are simulated.
256 devices in a mesh: dom: 64 (over z, x, core), rep: 4 (over y).
Axes of the slice: x: 4, y: 4, z: 8, core: 2. Of those that a mesh axis runs over, the one named last changes fastest.
Arguments:
- entities: bfloat16 [65536, 512], P('dom'), may hold values from -60 to 60
- relations: bfloat16 [4, 512, 512], replicated, may hold values from -2 to 2
- head_local: int32 [131072], P(('dom', 'rep')), may hold values from 0 to 1023
- rel_ids: int32 [131072], P(('dom', 'rep')), may hold values from 0 to 3
- tail_part: int32 [131072, 1], P(('dom', 'rep')), may hold values from 0 to 63; in each aligned block of 512 rows (0 to 511, 512 to 1023, ...) at most 16 rows name the same one
- tail_local: int32 [131072], P(('dom', 'rep')), may hold values from 0 to 1023
- neg_local: int32 [2048], P('dom'), may hold values from 0 to 1023
Outputs:
- entity_grad: float32 [65536, 512], P('dom')
- relation_grad: float32 [4, 512, 512], replicated
- edge_loss: float32 [131072], P(('dom', 'rep'))
Inputs may be any that keep to these rules, and one draw needn't show every extreme that they name: `tail_part`: in the 512 edges of one device no partition is named by more than 16 edges, a bound that some block reaches.
All inputs are finite; a program needn't handle non-finite values.
Results may differ from a plain program's by a relative error of at most 0.012.
The roundings to bfloat16 on the way count: a program that leaves them out, or rounds other values in their place, can miss the bound.
Values may be sent and summed in bfloat16 or wider, within the bound.
A program may use at most 64 MiB of HBM per device.

v0:
```python
import math
import jax
import jax.numpy as jnp
from jax import lax
from jax.sharding import PartitionSpec as P

D = 512


def local(entities, relations, head_local, rel_ids, tail_part, tail_local, neg_local):
    factor = 1.0 / math.sqrt(D)
    ent_dev = entities.shape[0]
    columns = entities.shape[1]
    edge_count = head_local.shape[0]
    part_count = lax.axis_size("dom")
    capacity = 2 * edge_count // part_count
    slot_count = part_count * capacity
    relation_count = relations.shape[0]
    head_rows = jnp.take(entities, head_local, axis=0)
    selectors = [(rel_ids == relation)[:, None] for relation in range(relation_count)]
    query_sum = jnp.zeros((edge_count, columns), jnp.float32)
    for relation in range(relation_count):
        picked = jnp.where(selectors[relation], head_rows, jnp.zeros_like(head_rows))
        query_sum = query_sum + jnp.dot(
            picked, relations[relation], preferred_element_type=jnp.float32
        )
    queries = query_sum.astype(jnp.bfloat16)
    target = tail_part[:, 0]
    target_hot = (target[:, None] == jnp.arange(part_count, dtype=jnp.int32)[None, :]).astype(
        jnp.int32
    )
    earlier = jnp.cumsum(target_hot, axis=0) - target_hot
    position = jnp.sum(earlier * target_hot, axis=1)
    slot_index = target * capacity + position
    slot_match = (slot_index[None, :] == jnp.arange(slot_count, dtype=jnp.int32)[:, None]).astype(
        jnp.int32
    )
    filled = jnp.sum(slot_match, axis=1) > 0
    source = jnp.sum(slot_match * jnp.arange(edge_count, dtype=jnp.int32)[None, :], axis=1)
    send_ids = jnp.where(filled, jnp.take(tail_local, source, axis=0), 0).reshape(
        part_count, capacity
    )
    recv_ids = lax.all_to_all(send_ids, "dom", split_axis=0, concat_axis=0, tiled=True)
    looked_up = jnp.take(entities, recv_ids.reshape(-1), axis=0).reshape(
        part_count, capacity, columns
    )
    returned = lax.all_to_all(looked_up, "dom", split_axis=0, concat_axis=0, tiled=True)
    tail_embed = jnp.take(returned.reshape(slot_count, columns), slot_index, axis=0)
    own_negs = jnp.take(entities, neg_local, axis=0)
    negatives = lax.all_gather(own_negs, "dom", axis=0, tiled=True)
    positive = (
        jnp.sum(queries.astype(jnp.float32) * tail_embed.astype(jnp.float32), axis=1) * factor
    )
    scores = (
        lax.dot_general(
            queries, negatives, (((1,), (1,)), ((), ())), preferred_element_type=jnp.float32
        )
        * factor
    )
    row_max = jnp.maximum(positive, jnp.max(scores, axis=1))
    exp_pos = jnp.exp(positive - row_max)
    exp_neg = jnp.exp(scores - row_max[:, None])
    partition_sum = exp_pos + jnp.sum(exp_neg, axis=1)
    edge_loss = jnp.log(partition_sum) + row_max - positive
    prob_pos = exp_pos / partition_sum
    prob_neg = (exp_neg / partition_sum[:, None]).astype(jnp.bfloat16)
    mixed = jnp.dot(prob_neg, negatives, preferred_element_type=jnp.float32)
    query_grad = (
        factor * ((prob_pos - 1.0)[:, None] * tail_embed.astype(jnp.float32) + mixed)
    ).astype(jnp.bfloat16)
    tail_grad = factor * (prob_pos - 1.0)[:, None] * queries.astype(jnp.float32)
    neg_grad = factor * lax.dot_general(
        prob_neg, queries, (((0,), (0,)), ((), ())), preferred_element_type=jnp.float32
    )
    head_grad = jnp.zeros((edge_count, columns), jnp.float32)
    rel_terms = []
    for relation in range(relation_count):
        picked_grad = jnp.where(selectors[relation], query_grad, jnp.zeros_like(query_grad))
        head_grad = head_grad + lax.dot_general(
            picked_grad,
            relations[relation],
            (((1,), (1,)), ((), ())),
            preferred_element_type=jnp.float32,
        )
        picked_rows = jnp.where(selectors[relation], head_rows, jnp.zeros_like(head_rows))
        rel_terms.append(
            lax.dot_general(
                picked_rows,
                query_grad,
                (((0,), (0,)), ((), ())),
                preferred_element_type=jnp.float32,
            )
        )
    relation_grad = lax.psum(jnp.stack(rel_terms), ("dom", "rep"))
    grad_send = jnp.where(filled[:, None], jnp.take(tail_grad, source, axis=0), 0.0)
    grad_recv = lax.all_to_all(
        grad_send.reshape(part_count, capacity, columns),
        "dom",
        split_axis=0,
        concat_axis=0,
        tiled=True,
    )
    owned = lax.psum_scatter(neg_grad, "dom", scatter_dimension=0, tiled=True)
    target_ids = jnp.concatenate([head_local, recv_ids.reshape(-1), neg_local])
    target_rows = jnp.concatenate(
        [head_grad, grad_recv.reshape(slot_count, columns), owned], axis=0
    )
    block_rows = min(512, ent_dev)
    block_count = ent_dev // block_rows

    def add_block(start):
        hot = (
            target_ids[None, :] == (start + jnp.arange(block_rows, dtype=jnp.int32))[:, None]
        ).astype(jnp.float32)
        return jnp.dot(
            hot, target_rows, precision=lax.Precision.HIGHEST, preferred_element_type=jnp.float32
        )

    local_grad = lax.map(add_block, jnp.arange(block_count, dtype=jnp.int32) * block_rows).reshape(
        ent_dev, columns
    )
    entity_grad = lax.psum(local_grad, "rep")
    return (entity_grad, relation_grad, edge_loss)


def solution(mesh):
    return jax.shard_map(
        local,
        mesh=mesh,
        in_specs=(
            P("dom", None),
            P(),
            P(("dom", "rep")),
            P(("dom", "rep")),
            P(("dom", "rep"), None),
            P(("dom", "rep")),
            P("dom"),
        ),
        out_specs=(P("dom", None), P(), P(("dom", "rep"))),
        check_vma=False,
    )
```

profile of v0, /device:TPU:1, one launch (start us, length us, event | category | flops | bytes accessed | tf_op | source)
XLA Modules:
  0.0 596.3 jit_solution(15604910715601647900)
XLA Ops:
  10.7 1.2 reduce-window.6
  14.5 6.9 %gather_fusion = s32[1024]{0:T(1024)S(1)} fusion(s32[512]{0:T(512)S(1)} %copy-done.1, s32[1024]{0:T(1024)S(1)} %broadcast_clamp_fusion.1), kind=kCustom, calls=%fused_computation.2 | custom fusion | bytes 12288 | tf_op jit(solution)/shard_map/jit(_take)/gather | solution.py:40
  21.5 22.2 %all_to_all.16 = s32[64,1,16]{2,1,0:T(1,128)S(1)} all-to-all(s32[64,1,16]{2,1,0:T(1,128)S(1)} %bitcast.90), channel_id=1, replica_groups=mesh['dom'=64,'rep'=4] {'dom'}, dimensions={0} | all-to-all | bytes 8192 | tf_op jit(solution)/shard_map/all_to_all | solution.py:43
  43.8 4.0 gather_fusion.1
  47.8 1.2 broadcast_select_fusion
  49.0 4.8 all-to-all-start.1
  54.0 2.0 gather_fusion.4
  56.3 1.7 fusion.23
  58.7 1.5 convolution_add_fusion.4
  60.1 24.6 %all-to-all-done.1 = bf16[64,16,512]{2,1,0:T(8,128)(2,1)S(1)} async-done(((bf16[64,16,512]{2,1,0:T(8,128)(2,1)}), bf16[64,16,512]{2,1,0:T(8,128)(2,1)S(1)}, u32[]{:S(2)}, u32[]{:S(2)}) %all-to-all-start.1) | async-done | bytes 1048608 | tf_op jit(solution)/shard_map/all_to_all | solution.py:47
  84.7 2.0 gather_fusion.5
  86.9 2.1 fusion.14
  89.0 5.9 all-gather.2.cloned.1.call-done
  94.9 3.0 multiply_reduce_fusion
  100.2 1.3 copy-done.2
  101.5 3.3 convolution_multiply_fusion
  105.5 4.9 gather_fusion.3
  110.3 2.7 select_select_fusion
  113.1 6.7 %all-to-all-start.2 = ((f32[64,16,512]{2,1,0:T(8,128)}), f32[64,16,512]{2,1,0:T(8,128)}, u32[]{:S(2)}, u32[]{:S(2)}) async-start(f32[64,16,512]{2,1,0:T(8,128)} %select_select_fusion), calls=%async_computation.2 | async-start | bytes 4194304 | tf_op jit(solution)/shard_map/all_to_all | solution.py:96
  121.4 3.1 fusion.12
  126.4 2.4 pad_maximum_fusion
  129.9 1.7 fusion.21
  133.2 36.2 %all-to-all-done.2 = f32[64,16,512]{2,1,0:T(8,128)} async-done(((f32[64,16,512]{2,1,0:T(8,128)}), f32[64,16,512]{2,1,0:T(8,128)}, u32[]{:S(2)}, u32[]{:S(2)}) %all-to-all-start.2) | async-done | bytes 2097184 | tf_op jit(solution)/shard_map/all_to_all | solution.py:96
  169.4 71.1 %reduce-scatter.2.cloned.1.call-done = f32[32,512]{1,0:T(8,128)} async-done(((f32[2048,512]{1,0:T(8,128)}), f32[32,512]{1,0:T(8,128)}) %reduce-scatter.2.cloned.1.call-update) | async-done | bytes 65552 | tf_op jit(solution)/shard_map/reduce_scatter | solution.py:103
  240.4 3.6 pad_maximum_fusion.1
  244.1 14.5 %while.10 = (s32[]{:T(128)}, f32[2,512,512]{2,1,0:T(8,128)}, s32[1568]{0:T(1024)S(1)}, s32[2]{0:T(128)S(1)}, f32[1568,512]{1,0:T(8,128)}, /*index=5*/s32[]{:T(128)}) while((s32[]{:T(128)}, f32[2,512,512]{2,1,0:T(8,128)}, s32[1568]{0:T(1024)S(1)}, s32[2]{0:T(128)S(1)}, f32[1568,512]{1,0:T(8,128)}, /*index=5*/s32[]{:T(128)}) %tuple.34), condition=%wide.region_10.12_spmd, body=%wide.region_9.11_spmd.sunk | while | flops 4933304832 | bytes 4270305 | solution.py:119
  245.2 6.1 %fusion.94 = f32[2,512,512]{2,1,0:T(8,128)} fusion(f32[2,512,512]{2,1,0:T(8,128)} %get-tuple-element.97, s32[]{:T(128)S(6)} %copy.37, f32[1568,512]{1,0:T(8,128)} %get-tuple-element.106, s32[1568]{0:T(1024)S(1)} %get-tuple-element.104, s32[512]{0:T(512)S(1)} %iota_add_fusion.2), kind=kOutput, calls=%fused_computation.11.clone.1 | convolution fusion | flops 4933304320 | bytes 4268164 | tf_op jit(solution)/shard_map/while/body/eval_jaxpr/dot_general | solution.py:115
  252.5 6.1 %fusion.94 = f32[2,512,512]{2,1,0:T(8,128)} fusion(f32[2,512,512]{2,1,0:T(8,128)} %get-tuple-element.97, s32[]{:T(128)S(6)} %copy.37, f32[1568,512]{1,0:T(8,128)} %get-tuple-element.106, s32[1568]{0:T(1024)S(1)} %get-tuple-element.104, s32[512]{0:T(512)S(1)} %iota_add_fusion.2), kind=kOutput, calls=%fused_computation.11.clone.1 | convolution fusion | flops 4933304320 | bytes 4268164 | tf_op jit(solution)/shard_map/while/body/eval_jaxpr/dot_general | solution.py:115
  258.6 258.9 %all-reduce.5.cloned.1.call-done = f32[4,512,512]{2,1,0:T(8,128)} async-done(((f32[4,512,512]{2,1,0:T(8,128)}), f32[4,512,512]{2,1,0:T(8,128)}) %all-reduce.5.cloned.1.call-update) | async-done | bytes 4194320 | tf_op jit(solution)/shard_map/psum | solution.py:94
  517.5 67.0 %all-reduce.3.cloned.1.call-done = f32[1024,512]{1,0:T(8,128)} async-done(((f32[1024,512]{1,0:T(8,128)}), f32[1024,512]{1,0:T(8,128)}) %all-reduce.3.cloned.1.call-update) | async-done | bytes 2097168 | tf_op jit(solution)/shard_map/psum | solution.py:122
  584.5 3.2 copy.45
  587.7 2.0 copy.46
  (94 shorter events, 18.9 us)
Async XLA Ops:
  7.2 1.5 copy-start
  7.2 7.4 %copy-start.1 = (s32[512]{0:T(512)S(1)}, s32[512]{0:T(512)}, u32[]{:S(2)}) copy-start(s32[512]{0:T(512)} %param.16) | copy-start | bytes 6148
  7.2 87.7 %all-gather.2.cloned.1.call-start = ((), (), s32[]{:S(2)}) async-start(), calls=%async_computation.4 | async-start | bytes 2129920 | tf_op jit(solution)/shard_map/all_gather | solution.py:50
  47.8 6.2 %copy-start.12 = (s32[512]{0:T(512)S(1)}, s32[512]{0:T(512)}, u32[]{:S(2)}) copy-start(s32[512]{0:T(512)} %param.13) | copy-start | bytes 6148
  49.0 35.7 %all-to-all-start.1 = ((bf16[64,16,512]{2,1,0:T(8,128)(2,1)}), bf16[64,16,512]{2,1,0:T(8,128)(2,1)S(1)}, u32[]{:S(2)}, u32[]{:S(2)}) async-start(bf16[64,16,512]{2,1,0:T(8,128)(2,1)} %broadcast_select_fusion), calls=%async_computation.1 | async-start | bytes 2097152 | tf_op jit(solution)/shard_map/all_to_all | solution.py:47
  53.8 186.7 %reduce-scatter.2.cloned.1.call-start = ((), (), s32[]{:S(2)}) async-start(), calls=%async_computation.5 | async-start | bytes 4259840 | tf_op jit(solution)/shard_map/reduce_scatter | solution.py:103
  54.0 2.3 copy-start.13
  56.2 30.7 %copy-start.4 = (bf16[512,512]{0,1:T(8,128)(2,1)}, bf16[512,512]{0,1:T(8,128)(2,1)S(1)}, u32[]{:S(2)}) copy-start(bf16[512,512]{0,1:T(8,128)(2,1)S(1)} %copy.27) | copy-start | bytes 1572868
  56.2 1.9 copy-start.9
  86.9 2.1 copy-start.11
  100.2 1.3 copy-start.2
  113.1 8.3 %copy-start.14 = (s32[32]{0:T(128)S(1)}, s32[32]{0:T(128)}, u32[]{:S(2)}) copy-start(s32[32]{0:T(128)} %param.17) | copy-start | bytes 388
  113.1 8.3 %copy-start.3 = (bf16[512,2048]{1,0:T(8,128)(2,1)S(1)}, bf16[512,2048]{1,0:T(8,128)(2,1)}, u32[]{:S(2)}) copy-start(bf16[512,2048]{1,0:T(8,128)(2,1)} %copy-done.2) | copy-start | bytes 6291460
  113.1 56.3 %all-to-all-start.2 = ((f32[64,16,512]{2,1,0:T(8,128)}), f32[64,16,512]{2,1,0:T(8,128)}, u32[]{:S(2)}, u32[]{:S(2)}) async-start(f32[64,16,512]{2,1,0:T(8,128)} %select_select_fusion), calls=%async_computation.2 | async-start | bytes 4194304 | tf_op jit(solution)/shard_map/all_to_all | solution.py:96
  119.8 397.7 %all-reduce.5.cloned.1.call-start = ((), (), s32[]{:S(2)}) async-start(), calls=%async_computation.7 | async-start | bytes 8388608 | tf_op jit(solution)/shard_map/psum | solution.py:94
  121.4 3.1 copy-start.5
  124.5 1.4 copy-start.6
  128.8 1.1 copy-start.7
  128.9 455.6 %all-reduce.3.cloned.1.call-start = ((), (), s32[]{:S(2)}) async-start(), calls=%async_computation.6 | async-start | bytes 4194304 | tf_op jit(solution)/shard_map/psum | solution.py:122
  129.9 1.8 copy-start.10
  584.5 3.2 copy-start.8
Sparse Core Ops, SparseCore 0:
  10.8 84.0 all-gather.1
  104.9 135.4 reduce-scatter.1
  246.8 270.6 all-reduce.4
  520.3 64.1 all-reduce.2
where the time goes:
time: 597 us; the launch traced here: 596 us
  waiting for transfers between devices  464 us (78%)
  matrix products  32.5 us (5%)
  local copies, waits for them, and re-layouts  31.2 us (5%)
  blocking collectives  22.2 us (4%)
  other arithmetic  20.5 us (3%)
  between operations  14.2 us (2%)
  starting transfers between devices  12 us (2%)
    psum x1, waiting for transfers between devices, local(): relation_grad = lax.psum(jnp.stack(rel_terms), ('dom', 'rep'))  259 us
    reduce_scatter x1, waiting for transfers between devices, local(): owned = lax.psum_scatter(neg_grad, 'dom', scatter_dimension=0, tiled=True)  71.1 us
    psum x1, waiting for transfers between devices, local(): entity_grad = lax.psum(local_grad, 'rep')  67 us
    all_to_all x1, waiting for transfers between devices, local(): lax.all_to_all(grad_send.reshape(part_count, capacity, columns), 'dom', s...  36.2 us
    all_to_all x1, waiting for transfers between devices, local(): lax.all_to_all(looked_up, 'dom', split_axis=0, concat_axis=0, tiled=True)  24.6 us
    all_to_all x1, blocking collectives, local(): lax.all_to_all(send_ids, 'dom', split_axis=0, concat_axis=0, tiled=True)  22.2 us
    dot_general x2, matrix products, add_block(): jnp.dot(hot, target_rows, precision=lax.Precision.HIGHEST, preferred_elem...  12.3 us
  transfers between devices with their start and end apart: 6, of which 6 were waited for; matrix products, arithmetic and copies ran while one was open for 11% of the time, Pallas kernels for 0%

commit v1 on v0

--- a/solution.py
+++ b/solution.py
@@ -119,7 +119,7 @@
     local_grad = lax.map(add_block, jnp.arange(block_count, dtype=jnp.int32) * block_rows).reshape(
         ent_dev, columns
     )
-    entity_grad = lax.psum(local_grad, "rep")
+    entity_grad = jnp.sum(lax.all_gather(local_grad, "rep"), axis=0)
     return (entity_grad, relation_grad, edge_loss)
 
 

time: 597 us -> 635 us (1.064)
  waiting for transfers between devices: 464 us -> 497 us
  other arithmetic: 20.5 us -> 27.7 us
    all_gather x0 -> x1, waiting for transfers between devices: none -> 83.8 us  [local(): entity_grad = jnp.sum(lax.all_gather(local_grad, 'rep'), axis=0)]
    psum x1 -> x0, waiting for transfers between devices: 67 us -> none  [local(): entity_grad = lax.psum(local_grad, 'rep')]
    psum x1, waiting for transfers between devices: 259 us -> 269 us  [local(): relation_grad = lax.psum(jnp.stack(rel_terms), ('dom', 'rep'))]
    all_to_all x1, waiting for transfers between devices: 36.2 us -> 42.8 us  [local(): lax.all_to_all(grad_send.reshape(part_count, capacity, columns), 'dom', s...]
  transfers between devices with their start and end apart: 6 -> 6, of which waited for: 6 -> 6; matrix products, arithmetic and copies ran while one was open for 11% -> 8% of each run, Pallas kernels for 0% -> 0%
where the time goes in v1:
time: 635 us; the launch traced here: 634 us
  waiting for transfers between devices  497 us (78%)
  local copies, waits for them, and re-layouts  30.6 us (5%)
  matrix products  30 us (5%)
  other arithmetic  27.7 us (4%)
  blocking collectives  22.2 us (3%)
  between operations  14.2 us (2%)
  starting transfers between devices  12.2 us (2%)
    psum x1, waiting for transfers between devices, local(): relation_grad = lax.psum(jnp.stack(rel_terms), ('dom', 'rep'))  269 us
    all_gather x1, waiting for transfers between devices, local(): entity_grad = jnp.sum(lax.all_gather(local_grad, 'rep'), axis=0)  83.8 us
    reduce_scatter x1, waiting for transfers between devices, local(): owned = lax.psum_scatter(neg_grad, 'dom', scatter_dimension=0, tiled=True)  69.1 us
    all_to_all x1, waiting for transfers between devices, local(): lax.all_to_all(grad_send.reshape(part_count, capacity, columns), 'dom', s...  42.8 us
    all_to_all x1, waiting for transfers between devices, local(): lax.all_to_all(looked_up, 'dom', split_axis=0, concat_axis=0, tiled=True)  25.9 us
    all_to_all x1, blocking collectives, local(): lax.all_to_all(send_ids, 'dom', split_axis=0, concat_axis=0, tiled=True)  22.2 us
  transfers between devices with their start and end apart: 6, of which 6 were waited for; matrix products, arithmetic and copies ran while one was open for 8% of the time, Pallas kernels for 0%

profile of v1, /device:TPU:1, one launch (start us, length us, event | category | flops | bytes accessed | tf_op | source)
XLA Modules:
  0.0 633.6 jit_solution(1067248375319757793)
XLA Ops:
  10.7 1.2 reduce-window.6
  14.6 6.9 %gather_fusion = s32[1024]{0:T(1024)S(1)} fusion(s32[512]{0:T(512)S(1)} %copy-done.2, s32[1024]{0:T(1024)S(1)} %broadcast_clamp_fusion.1), kind=kCustom, calls=%fused_computation.2 | custom fusion | bytes 12288 | tf_op jit(solution)/shard_map/jit(_take)/gather | solution.py:40
  21.5 22.2 %all_to_all.16 = s32[64,1,16]{2,1,0:T(1,128)S(1)} all-to-all(s32[64,1,16]{2,1,0:T(1,128)S(1)} %bitcast.90), channel_id=1, replica_groups=mesh['dom'=64,'rep'=4] {'dom'}, dimensions={0} | all-to-all | bytes 8192 | tf_op jit(solution)/shard_map/all_to_all | solution.py:43
  43.8 4.0 gather_fusion.1
  47.8 1.2 broadcast_select_fusion
  49.0 4.8 all-to-all-start.1
  54.0 2.0 gather_fusion.4
  56.3 1.7 fusion.23
  59.2 25.9 %all-to-all-done.1 = bf16[64,16,512]{2,1,0:T(8,128)(2,1)S(1)} async-done(((bf16[64,16,512]{2,1,0:T(8,128)(2,1)}), bf16[64,16,512]{2,1,0:T(8,128)(2,1)S(1)}, u32[]{:S(2)}, u32[]{:S(2)}) %all-to-all-start.1) | async-done | bytes 1048608 | tf_op jit(solution)/shard_map/all_to_all | solution.py:47
  85.0 2.0 gather_fusion.5
  87.2 1.8 fusion.14
  89.0 6.3 all-gather.3.cloned.1.call-done
  95.3 3.0 multiply_reduce_fusion
  100.6 3.3 convolution_multiply_fusion
  104.1 1.1 convert_multiply_fusion.2
  105.2 1.6 copy.30
  106.8 4.9 gather_fusion.3
  111.7 2.8 select_select_fusion
  114.5 6.9 %all-to-all-start.2 = ((f32[64,16,512]{2,1,0:T(8,128)}), f32[64,16,512]{2,1,0:T(8,128)}, u32[]{:S(2)}, u32[]{:S(2)}) async-start(f32[64,16,512]{2,1,0:T(8,128)} %select_select_fusion), calls=%async_computation.2 | async-start | bytes 4194304 | tf_op jit(solution)/shard_map/all_to_all | solution.py:96
  123.0 3.1 fusion.12
  128.1 42.8 %all-to-all-done.2 = f32[64,16,512]{2,1,0:T(8,128)} async-done(((f32[64,16,512]{2,1,0:T(8,128)}), f32[64,16,512]{2,1,0:T(8,128)}, u32[]{:S(2)}, u32[]{:S(2)}) %all-to-all-start.2) | async-done | bytes 2097184 | tf_op jit(solution)/shard_map/all_to_all | solution.py:96
  170.9 69.1 %reduce-scatter.2.cloned.1.call-done = f32[32,512]{1,0:T(8,128)} async-done(((f32[2048,512]{1,0:T(8,128)}), f32[32,512]{1,0:T(8,128)}) %reduce-scatter.2.cloned.1.call-update) | async-done | bytes 65552 | tf_op jit(solution)/shard_map/reduce_scatter | solution.py:103
  240.0 3.6 pad_maximum_fusion.1
  243.6 14.7 %while.10 = (s32[]{:T(128)}, f32[2,512,512]{2,1,0:T(8,128)}, s32[1568]{0:T(1024)S(1)}, s32[2]{0:T(128)S(1)}, f32[1568,512]{1,0:T(8,128)}, /*index=5*/s32[]{:T(128)}) while((s32[]{:T(128)}, f32[2,512,512]{2,1,0:T(8,128)}, s32[1568]{0:T(1024)S(1)}, s32[2]{0:T(128)S(1)}, f32[1568,512]{1,0:T(8,128)}, /*index=5*/s32[]{:T(128)}) %tuple.34), condition=%wide.region_10.12_spmd, body=%wide.region_9.11_spmd.sunk | while | flops 4933304832 | bytes 4270305 | solution.py:119
  244.8 6.1 fusion.94
  252.2 6.1 fusion.94
  258.4 1.0 copy-done.4
  261.2 2.5 pad_maximum_fusion
  263.7 83.8 %all-gather.5.cloned.1.call-done = f32[4,1024,512]{2,1,0:T(8,128)} async-done(((f32[1,1024,512]{2,1,0:T(8,128)}), f32[4,1024,512]{2,1,0:T(8,128)}) %all-gather.5.cloned.1.call-update) | async-done | bytes 8388624 | tf_op jit(solution)/shard_map/all_gather | solution.py:122
  347.6 6.0 reduce_sum.68
  353.5 268.9 %all-reduce.2.cloned.1.call-done = f32[4,512,512]{2,1,0:T(8,128)} async-done(((f32[4,512,512]{2,1,0:T(8,128)}), f32[4,512,512]{2,1,0:T(8,128)}) %all-reduce.2.cloned.1.call-update) | async-done | bytes 4194320 | tf_op jit(solution)/shard_map/psum | solution.py:94
  622.4 4.7 copy.44
  (88 shorter events, 18.5 us)
Async XLA Ops:
  7.2 1.5 copy-start
  7.2 7.4 %copy-start.2 = (s32[512]{0:T(512)S(1)}, s32[512]{0:T(512)}, u32[]{:S(2)}) copy-start(s32[512]{0:T(512)} %param.16) | copy-start | bytes 6148
  7.2 88.1 %all-gather.3.cloned.1.call-start = ((), (), s32[]{:S(2)}) async-start(), calls=%async_computation.4 | async-start | bytes 2129920 | tf_op jit(solution)/shard_map/all_gather | solution.py:50
  47.8 6.2 copy-start.9
  49.0 36.0 %all-to-all-start.1 = ((bf16[64,16,512]{2,1,0:T(8,128)(2,1)}), bf16[64,16,512]{2,1,0:T(8,128)(2,1)S(1)}, u32[]{:S(2)}, u32[]{:S(2)}) async-start(bf16[64,16,512]{2,1,0:T(8,128)(2,1)} %broadcast_select_fusion), calls=%async_computation.1 | async-start | bytes 2097152 | tf_op jit(solution)/shard_map/all_to_all | solution.py:47
  53.8 186.2 %reduce-scatter.2.cloned.1.call-start = ((), (), s32[]{:S(2)}) async-start(), calls=%async_computation.5 | async-start | bytes 4259840 | tf_op jit(solution)/shard_map/reduce_scatter | solution.py:103
  54.0 2.3 copy-start.10
  56.2 31.0 %copy-start.3 = (bf16[512,512]{0,1:T(8,128)(2,1)}, bf16[512,512]{0,1:T(8,128)(2,1)S(1)}, u32[]{:S(2)}) copy-start(bf16[512,512]{0,1:T(8,128)(2,1)S(1)} %copy.27) | copy-start | bytes 1572868
  56.2 1.9 copy-start.5
  87.2 1.8 copy-start.7
  114.5 8.5 %copy-start.11 = (s32[32]{0:T(128)S(1)}, s32[32]{0:T(128)}, u32[]{:S(2)}) copy-start(s32[32]{0:T(128)} %param.17) | copy-start | bytes 388
  114.5 8.5 %copy-start.8 = (bf16[512,512]{0,1:T(8,128)(2,1)S(1)}, bf16[512,512]{0,1:T(8,128)(2,1)}, u32[]{:S(2)}) copy-start(bf16[512,512]{0,1:T(8,128)(2,1)} %copy-done.7) | copy-start | bytes 1572868
  114.5 56.5 %all-to-all-start.2 = ((f32[64,16,512]{2,1,0:T(8,128)}), f32[64,16,512]{2,1,0:T(8,128)}, u32[]{:S(2)}, u32[]{:S(2)}) async-start(f32[64,16,512]{2,1,0:T(8,128)} %select_select_fusion), calls=%async_computation.2 | async-start | bytes 4194304 | tf_op jit(solution)/shard_map/all_to_all | solution.py:96
  121.3 226.2 %all-gather.5.cloned.1.call-start = ((), (), s32[]{:S(2)}) async-start(), calls=%async_computation.6 | async-start | bytes 10485760 | tf_op jit(solution)/shard_map/all_gather | solution.py:122
  123.0 3.1 copy-start.6
  258.3 1.0 copy-start.4
  258.3 364.0 %all-reduce.2.cloned.1.call-start = ((), (), s32[]{:S(2)}) async-start(), calls=%async_computation.7 | async-start | bytes 8388608 | tf_op jit(solution)/shard_map/psum | solution.py:94
  622.4 4.7 copy-start.1
Sparse Core Ops, SparseCore 0:
  11.4 83.9 all-gather.2
  104.1 135.8 reduce-scatter.1
  258.4 89.0 all-gather.4
  354.4 267.9 all-reduce.1
